TPU v7x, 32 devices: a whole 2x2x4 slice. The times are simulated.
32 devices in a mesh: chan: 8 (over z, x), tm: 4 (over y, core).
Axes of the slice: x: 2, y: 2, z: 4, core: 2. Of those that a mesh axis runs over, the one named last changes fastest.
Arguments:
- samples: bfloat16 [2048, 131072], P('chan', 'tm'), may hold values from -6 to 6
- fir_taps: float32 [8, 4096], replicated, may hold values from -2 to 2
- beam_y: bfloat16 [2, 32, 32], replicated, may hold values from -0.75 to 0.75
- beam_x: bfloat16 [2, 64, 64], replicated, may hold values from -0.5 to 0.5
- delays: int32 [64, 2048], replicated, may hold values from 0 to 8, as said below
Outputs:
- series: float32 [2048, 32, 64], P('chan', 'tm')
Inputs may be any that keep to these rules, and one draw needn't show every extreme that they name: Each trial's delays come from a dispersion law: along a row they never rise with the channel index; the largest value is reached.
All inputs are finite; a program needn't handle non-finite values.
Results may differ from a plain program's by a relative error of at most 0.00068.
Values may be sent and summed in bfloat16 or wider, within the bound.
No kernel may reach another device: no remote copies, remote signals or barrier semaphores. Data moves between devices by JAX's collectives and lax.ppermute only.
A program may use at most 192 MiB of HBM per device.

v0:
```python
import math

import jax
import jax.numpy as jnp
from jax import lax
from jax.sharding import PartitionSpec as P


def shifted(array, axis, by):
    count = lax.axis_size(axis)
    pairs = [(i, i + by) for i in range(count) if 0 <= i + by < count]
    return lax.ppermute(array, axis, pairs)


def phase_table(rows_count, cols_count, period):
    row_index = jnp.arange(rows_count, dtype=jnp.int32)[:, None]
    col_index = jnp.arange(cols_count, dtype=jnp.int32)[None, :]
    angle = (row_index * col_index % period).astype(jnp.float32) * (2.0 * math.pi / period)
    return (jnp.cos(angle), jnp.sin(angle))


def transform(frames_rows, nfft):
    bits = nfft.bit_length() - 1
    first = 1 << bits // 2
    second = nfft // first
    rows_count = frames_rows.shape[0]
    shaped = frames_rows.reshape(rows_count, first, second)
    highest = lax.Precision.HIGHEST
    cos_one, sin_one = phase_table(first, first, first)
    section_real = jnp.einsum("rab,ak->rkb", shaped, cos_one, precision=highest)
    section_imag = -jnp.einsum("rab,ak->rkb", shaped, sin_one, precision=highest)
    cos_twist, sin_twist = phase_table(first, second, nfft)
    twist_real = section_real * cos_twist[None] + section_imag * sin_twist[None]
    twist_imag = section_imag * cos_twist[None] - section_real * sin_twist[None]
    cos_two, sin_two = phase_table(second, second // 2, second)
    out_real = jnp.einsum("rkb,bm->rmk", twist_real, cos_two, precision=highest) + jnp.einsum(
        "rkb,bm->rmk", twist_imag, sin_two, precision=highest
    )
    out_imag = jnp.einsum("rkb,bm->rmk", twist_imag, cos_two, precision=highest) - jnp.einsum(
        "rkb,bm->rmk", twist_real, sin_two, precision=highest
    )
    scale = 1.0 / math.sqrt(nfft)
    return (
        out_real.reshape(rows_count, nfft // 2) * scale,
        out_imag.reshape(rows_count, nfft // 2) * scale,
    )


def complex_product(weights, real_part, imag_part, form):
    w_real = weights[0]
    w_imag = weights[1]
    out_real = jnp.einsum(form, w_real, real_part, preferred_element_type=jnp.float32) - jnp.einsum(
        form, w_imag, imag_part, preferred_element_type=jnp.float32
    )
    out_imag = jnp.einsum(form, w_real, imag_part, preferred_element_type=jnp.float32) + jnp.einsum(
        form, w_imag, real_part, preferred_element_type=jnp.float32
    )
    return (out_real, out_imag)


def dedisperse(extended, delay_block, spec_dev, trials, scale):
    beam_count = extended.shape[2]

    def turn(shift_value, total):
        piece = lax.dynamic_slice_in_dim(extended, shift_value, spec_dev, 0)
        selector = (delay_block == shift_value).astype(jnp.bfloat16)
        return total + jnp.einsum(
            "scb,tc->bst", piece, selector, preferred_element_type=jnp.float32
        )

    summed = lax.fori_loop(
        0, spec_dev + 1, turn, jnp.zeros((beam_count, spec_dev, trials), jnp.float32)
    )
    return summed * scale


def on_device(samples, fir_taps, beam_y, beam_x, delays):
    dish_dev, total_points = samples.shape
    taps_count, nfft = fir_taps.shape
    spec_dev = total_points // nfft
    side_x = beam_x.shape[1]
    side_y = beam_y.shape[1]
    trials, channels = delays.shape
    frames = samples.reshape(dish_dev, spec_dev, nfft)
    history = shifted(frames[:, spec_dev - taps_count + 1 :, :], "tm", 1)
    extended_frames = jnp.concatenate([history, frames], axis=1)
    filtered = jnp.zeros((dish_dev, spec_dev, nfft), jnp.float32)
    for tap_index in range(taps_count):
        offset = taps_count - 1 - tap_index
        filtered = filtered + fir_taps[tap_index][None, None, :] * extended_frames[
            :, offset : offset + spec_dev, :
        ].astype(jnp.float32)
    frame_rows = filtered.reshape(dish_dev * spec_dev, nfft)
    volt_real, volt_imag = transform(frame_rows, nfft)
    volts = jnp.stack(
        [
            volt_real.reshape(dish_dev, spec_dev, nfft // 2),
            volt_imag.reshape(dish_dev, spec_dev, nfft // 2),
        ],
        axis=2,
    ).astype(jnp.bfloat16)
    gathered = lax.all_to_all(volts, "chan", split_axis=3, concat_axis=0, tiled=True)
    items = gathered.shape[1]
    chan_dev = gathered.shape[3]
    grid = gathered.reshape(side_x, side_y, items, 2, chan_dev)
    part_real, part_imag = complex_product(
        beam_y, grid[:, :, :, 0], grid[:, :, :, 1], "py,xync->ncxp"
    )
    part_real = part_real.astype(jnp.bfloat16)
    part_imag = part_imag.astype(jnp.bfloat16)
    form_real, form_imag = complex_product(beam_x, part_real, part_imag, "qx,ncxp->ncqp")
    power = (form_real * form_real + form_imag * form_imag).reshape(
        items, chan_dev, side_x * side_y
    )
    powers = (power - jnp.mean(power, axis=2, keepdims=True)).astype(jnp.bfloat16)
    scale = 1.0 / math.sqrt(channels)
    chan_dev = powers.shape[1]
    following = shifted(powers, "tm", -1)
    extended = jnp.concatenate([powers, following], axis=0)
    local_delays = lax.dynamic_slice_in_dim(delays, lax.axis_index("chan") * chan_dev, chan_dev, 1)
    return lax.psum_scatter(
        dedisperse(extended, local_delays, spec_dev, trials, scale),
        "chan",
        scatter_dimension=0,
        tiled=True,
    )


def solution(mesh):
    return jax.shard_map(
        on_device,
        mesh=mesh,
        in_specs=(P("chan", "tm"), P(), P(), P(), P()),
        out_specs=P("chan", "tm", None),
        check_vma=False,
    )
```

profile of v0, /device:TPU:0, one launch (start us, length us, event | category | flops | bytes accessed | tf_op | source)
XLA Modules:
  0.0 1550.2 jit_solution(6742614575479663688)
XLA Ops:
  6.5 0.0 copy-start
  6.5 0.0 reduce-scatter.2.cloned.1.call-start
  6.5 22.5 %copy.72 = bf16[256,32768]{0,1:T(8,128)(2,1)} copy(bf16[256,32768]{1,0:T(8,128)(2,1)} %param.7) | data formatting | bytes 33554432 | tf_op args[0]
  29.0 13.1 slice.88
  42.1 19.4 %copy.73 = bf16[256,7,4096]{2,0,1:T(8,128)(2,1)} copy(bf16[256,7,4096]{0,2,1:T(8,128)(2,1)} %slice.88) | data formatting | bytes 29360128 | tf_op jit(solution)/shard_map/slice | solution.py:85
  61.5 7.5 collective-permute-start
  69.1 0.1 fusion.68
  69.2 0.0 copy-done.5
  69.2 0.1 fusion.118
  69.3 16.7 %collective-permute-done = bf16[256,7,4096]{2,0,1:T(8,128)(2,1)} collective-permute-done((bf16[256,7,4096]{2,0,1:T(8,128)(2,1)}, bf16[256,7,4096]{2,0,1:T(8,128)(2,1)}, u32[]{:S(2)}, u32[]{:S(2)}) %collective-permute-start) | collective-permute-done | bytes 14680096 | tf_op jit(solution)/shard_map/ppermute | solution.py:12
  86.0 19.3 %copy.74 = bf16[256,7,4096]{0,2,1:T(8,128)(2,1)} copy(bf16[256,7,4096]{2,0,1:T(8,128)(2,1)} %collective-permute-done) | data formatting | bytes 29360128 | tf_op jit(solution)/shard_map/ppermute | solution.py:12
  105.4 53.0 %multiply_add_fusion = f32[256,8,4096]{0,2,1:T(8,128)} fusion(bf16[256,8,4096]{0,2,1:T(8,128)(2,1)} %bitcast.115, bf16[256,7,4096]{0,2,1:T(8,128)(2,1)} %copy.74, f32[4096]{0:T(1024)S(1)} %bitcast.124, f32[4096]{0:T(1024)S(1)} %bitcast.125, f32[4096]{0:T(1024)S(1)} %bitcast.119, f32[4096]{0:T(1024)S(1)} %bitcast.120, f32[4096]{0:T(1024)S(1)} %bitcast.121, ...), kind=kLoop, calls=%fused_computation.21 | loop fusion | flops 251658240 | bytes 65142784 | tf_op jit(solution)/shard_map/add | solution.py:90
  158.4 31.9 %copy.75 = f32[256,8,4096]{2,1,0:T(8,128)} copy(f32[256,8,4096]{0,2,1:T(8,128)} %multiply_add_fusion) | data formatting | bytes 67108864 | tf_op jit(solution)/shard_map/add | solution.py:90
  190.3 52.7 %reshape_reshape.3 = f32[2048,64,64]{2,1,0:T(8,128)} reshape(f32[256,8,4096]{2,1,0:T(8,128)} %copy.75) | data formatting | bytes 67108864 | tf_op jit(solution)/shard_map/reshape;reshape | solution.py:27
  243.0 50.9 %copy.76 = f32[2048,64,64]{0,1,2:T(8,128)} copy(f32[2048,64,64]{2,1,0:T(8,128)} %reshape_reshape.3) | data formatting | bytes 67108864 | tf_op jit(solution)/shard_map/reshape;reshape | solution.py:27
  293.9 37.1 %fusion.44 = f32[64,2048,64]{1,0,2:T(8,128)} fusion(f32[2048,64,64]{0,1,2:T(8,128)} %copy.76), kind=kOutput, calls=%fused_computation.71 | convolution fusion | flops 6442508288 | bytes 67108864 | tf_op jit(solution)/shard_map/rab,ak->rkb/dot_general | solution.py:31
  331.0 54.9 %add_bitcast_fusion = (f32[2048,64,64]{0,1,2:T(8,128)}, f32[2048,64,64]{0,1,2:T(8,128)}) fusion(f32[64,2048,64]{1,0,2:T(8,128)} %fusion.44, f32[64,64]{0,1:T(8,128)S(1)} %get-tuple-element.138, f32[64,64]{0,1:T(8,128)S(1)} %get-tuple-element.139, f32[2048,64,64]{0,1,2:T(8,128)} %copy.76), kind=kOutput, calls=%fused_computation.20 | convolution fusion | flops 6501228544 | bytes 134250496 | tf_op jit(solution)/shard_map/rab,ak->rkb/dot_general | solution.py:30
  385.9 45.8 %fusion.10 = f32[32,2048,64]{1,0,2:T(8,128)} fusion(f32[2048,64,64]{0,1,2:T(8,128)} %get-tuple-element.125), kind=kOutput, calls=%fused_computation.24 | convolution fusion | flops 3221254144 | bytes 50331648 | tf_op jit(solution)/shard_map/rkb,bm->rmk/dot_general | solution.py:36
  431.7 46.4 %fusion.8 = f32[32,2048,64]{1,0,2:T(8,128)} fusion(f32[2048,64,64]{0,1,2:T(8,128)} %get-tuple-element.125), kind=kOutput, calls=%fused_computation.22 | convolution fusion | flops 3221254144 | bytes 50331648 | tf_op jit(solution)/shard_map/rkb,bm->rmk/dot_general | solution.py:39
  478.1 49.3 %fusion.23 = bf16[2048,32,64]{0,1,2:T(8,128)(2,1)} fusion(f32[32,2048,64]{1,0,2:T(8,128)} %fusion.10, f32[2048,64,64]{0,1,2:T(8,128)} %get-tuple-element.124), kind=kOutput, calls=%fused_computation.46 | convolution fusion | flops 3233837056 | bytes 58720256 | tf_op jit(solution)/shard_map/rkb,bm->rmk/dot_general | solution.py:36
  527.4 29.4 %copy.80 = bf16[2048,32,64]{2,1,0:T(8,128)(2,1)} copy(bf16[2048,32,64]{0,1,2:T(8,128)(2,1)} %fusion.23) | data formatting | bytes 16777216 | tf_op jit(solution)/shard_map/mul | solution.py:44
  556.8 23.4 %mul.337 = bf16[256,8,1,2048]{3,1,0,2:T(8,128)(2,1)} reshape(bf16[2048,32,64]{2,1,0:T(8,128)(2,1)} %copy.80) | data formatting | bytes 16777216 | tf_op jit(solution)/shard_map/mul | solution.py:44
  580.3 48.1 %fusion.24 = bf16[2048,32,64]{0,1,2:T(8,128)(2,1)} fusion(f32[32,2048,64]{1,0,2:T(8,128)} %fusion.8, f32[2048,64,64]{0,1,2:T(8,128)} %get-tuple-element.124), kind=kOutput, calls=%fused_computation.47 | convolution fusion | flops 3233837056 | bytes 58720256 | tf_op jit(solution)/shard_map/rkb,bm->rmk/dot_general | solution.py:39
  628.4 29.2 %copy.83 = bf16[2048,32,64]{2,1,0:T(8,128)(2,1)} copy(bf16[2048,32,64]{0,1,2:T(8,128)(2,1)} %fusion.24) | data formatting | bytes 16777216 | tf_op jit(solution)/shard_map/mul | solution.py:45
  657.6 23.4 %mul.340 = bf16[256,8,1,2048]{3,1,0,2:T(8,128)(2,1)} reshape(bf16[2048,32,64]{2,1,0:T(8,128)(2,1)} %copy.83) | data formatting | bytes 16777216 | tf_op jit(solution)/shard_map/mul | solution.py:45
  681.0 13.7 pad_maximum_fusion.1
  694.7 25.6 %copy.84 = bf16[256,8,2,2048]{0,1,2,3:T(8,128)(2,1)} copy(bf16[256,8,2,2048]{3,1,0,2:T(8,128)(2,1)} %pad_maximum_fusion.1) | data formatting | bytes 33554432 | tf_op jit(solution)/shard_map/stack | solution.py:95
  720.3 324.9 %all_to_all.15 = bf16[256,8,2,2048]{0,1,2,3:T(8,128)(2,1)} all-to-all(bf16[256,8,2,2048]{0,1,2,3:T(8,128)(2,1)} %copy.84), channel_id=1, replica_groups=mesh['chan'=8,'tm'=4] {'chan'}, dimensions={3} | all-to-all | bytes 33554432 | tf_op jit(solution)/shard_map/all_to_all | solution.py:102
  1045.2 25.7 %copy.86 = bf16[8,256,8,2,256]{4,2,3,1,0:T(8,128)(2,1)} copy(bf16[8,256,8,2,256]{1,2,3,4,0:T(8,128)(2,1)} %bitcast.117) | data formatting | bytes 33554432 | tf_op jit(solution)/shard_map/all_to_all | solution.py:102
  1070.9 6.6 fusion.117
  1077.6 0.0 copy-start.2
  1077.6 0.0 copy-start.1
  1077.6 3.2 copy-done.2
  1080.8 0.0 copy-done.7
  1080.8 8.1 fusion.25
  1088.8 0.0 copy-done.1
  1088.8 8.1 fusion.26
  1096.9 13.7 fusion.39
  1110.7 0.0 copy-done.6
  1110.7 16.2 %fusion.27 = f32[8,256,32,64]{1,3,2,0:T(8,128)} fusion(bf16[8,256,64,32]{1,3,0,2:T(8,128)(2,1)} %fusion.39, bf16[2,64,64]{2,1,0:T(8,128)(2,1)S(1)} %copy-done.6), kind=kOutput, calls=%fused_computation.52 | convolution fusion | flops 536870912 | bytes 25182208 | tf_op jit(solution)/shard_map/qx,ncxp->ncqp/dot_general | solution.py:52
  1126.9 0.0 copy-done.3
  1126.9 12.3 fusion.29
  1139.1 13.7 fusion.38
  1152.9 16.0 %fusion.31 = f32[8,256,32,64]{1,3,2,0:T(8,128)} fusion(bf16[8,256,64,32]{1,3,0,2:T(8,128)(2,1)} %fusion.38, bf16[2,64,64]{2,1,0:T(8,128)(2,1)S(1)} %copy-done.6), kind=kOutput, calls=%fused_computation.56 | convolution fusion | flops 536870912 | bytes 25182208 | tf_op jit(solution)/shard_map/qx,ncxp->ncqp/dot_general | solution.py:52
  1168.8 0.0 copy-done.4
  1168.9 23.3 %fusion.119 = (f32[8,256]{1,0:T(8,128)S(1)}, f32[8,256,64,32]{1,2,3,0:T(8,128)}) fusion(f32[8,256,32,64]{1,3,2,0:T(8,128)} %fusion.29, bf16[8,256,64,32]{1,3,0,2:T(8,128)(2,1)S(1)} %copy-done.4, bf16[2,64,64]{2,1,0:T(8,128)(2,1)S(1)} %copy-done.6, f32[8,256,32,64]{1,3,2,0:T(8,128)} %fusion.31, f32[8,256,32,64]{1,3,2,0:T(8,128)} %fusion.27), kind=kOutput, calls=%fused_computation.146 | convolution fusion | flops 562034688 | bytes 75522048 | tf_op jit(solution)/shard_map/qx,ncxp->ncqp/dot_general | solution.py:55
  1192.2 15.2 copy.93
  1207.4 4.9 fusion.22
  1212.3 1.3 collective-permute-start.1
  1213.6 60.8 %collective-permute-done.1 = bf16[8,256,2048]{1,2,0:T(8,128)(2,1)} collective-permute-done((bf16[8,256,2048]{1,2,0:T(8,128)(2,1)}, bf16[8,256,2048]{1,2,0:T(8,128)(2,1)}, u32[]{:S(2)}, u32[]{:S(2)}) %collective-permute-start.1) | collective-permute-done | bytes 8388640 | tf_op jit(solution)/shard_map/ppermute | solution.py:12
  1274.5 13.7 pad_maximum_fusion.2
  1288.2 82.9 %while.14 = (s32[]{:T(128)}, f32[2048,8,64]{0,2,1:T(8,128)}, s32[64,256]{1,0:T(8,128)S(1)}, bf16[16,256,2048]{1,2,0:T(8,128)(2,1)}, s32[]{:T(128)}, /*index=5*/s32[]{:T(128)}) while((s32[]{:T(128)}, f32[2048,8,64]{0,2,1:T(8,128)}, s32[64,256]{1,0:T(8,128)S(1)}, bf16[16,256,2048]{1,2,0:T(8,128)(2,1)}, s32[]{:T(128)}, ...), condition=%wide.region_2.3_spmd.clone, body=%wide.region_1.2_spmd.clone.sunk | while | flops 538984448 | bytes 16843852 | solution.py:71
  1288.2 8.1 bitcast_add_fusion.2
  1296.2 9.5 bitcast_add_fusion.2
  1305.7 9.5 bitcast_add_fusion.2
  1315.2 9.5 bitcast_add_fusion.2
  1324.7 9.3 bitcast_add_fusion.2
  1334.0 9.3 bitcast_add_fusion.2
  1343.2 9.3 bitcast_add_fusion.2
  1352.5 9.3 bitcast_add_fusion.2
  1361.8 9.3 bitcast_add_fusion.2
  1371.1 4.9 broadcast_multiply_fusion
  1376.0 0.0 reduce-scatter.2.cloned.1.call-update
  1376.0 167.2 %reduce-scatter.2.cloned.1.call-done = f32[256,8,64]{0,2,1:T(8,128)} async-done(((f32[2048,8,64]{0,2,1:T(8,128)}), f32[256,8,64]{0,2,1:T(8,128)}) %reduce-scatter.2.cloned.1.call-update) | async-done | bytes 524304 | tf_op jit(solution)/shard_map/reduce_scatter | solution.py:121
  (9 shorter events, 0.0 us)
Async XLA Ops:
  6.5 1207.1 %copy-start = (s32[64,2048]{1,0:T(8,128)S(1)}, s32[64,2048]{1,0:T(8,128)}, u32[]{:S(2)}) copy-start(s32[64,2048]{1,0:T(8,128)} %param.11) | copy-start | bytes 1572868
  6.5 1536.6 %reduce-scatter.2.cloned.1.call-start = ((), (), s32[]{:S(2)}) async-start(), calls=%async_computation.2 | async-start | bytes 4718592 | tf_op jit(solution)/shard_map/reduce_scatter | solution.py:121
  42.1 27.1 %copy-start.5 = (f32[8,4096]{1,0:T(8,128)S(1)}, f32[8,4096]{1,0:T(8,128)}, u32[]{:S(2)}) copy-start(f32[8,4096]{1,0:T(8,128)} %param.8) | copy-start | bytes 393220
  61.5 24.5 %collective-permute-start = (bf16[256,7,4096]{2,0,1:T(8,128)(2,1)}, bf16[256,7,4096]{2,0,1:T(8,128)(2,1)}, u32[]{:S(2)}, u32[]{:S(2)}) collective-permute-start(bf16[256,7,4096]{2,0,1:T(8,128)(2,1)} %copy.73), channel_id=1, source_target_pairs={{0,1},{1,2},{2,3},{4,5},{5,6},{6,7},{8,9},{9,10},{10,11},{12,13},{... | collective-permute-start | bytes 44040200 | tf_op jit(solution)/shard_map/ppermute | solution.py:12
  1070.9 9.8 copy-start.7
  1077.6 3.2 copy-start.2
  1077.6 11.3 copy-start.1
  1096.9 13.8 copy-start.6
  1110.7 16.2 %copy-start.3 = (bf16[8,256,64,32]{1,3,0,2:T(8,128)(2,1)S(1)}, bf16[8,256,64,32]{1,3,0,2:T(8,128)(2,1)}, u32[]{:S(2)}) copy-start(bf16[8,256,64,32]{1,3,0,2:T(8,128)(2,1)} %fusion.39) | copy-start | bytes 25165828
  1152.9 16.0 %copy-start.4 = (bf16[8,256,64,32]{1,3,0,2:T(8,128)(2,1)S(1)}, bf16[8,256,64,32]{1,3,0,2:T(8,128)(2,1)}, u32[]{:S(2)}) copy-start(bf16[8,256,64,32]{1,3,0,2:T(8,128)(2,1)} %fusion.38) | copy-start | bytes 25165828
  1212.3 62.2 %collective-permute-start.1 = (bf16[8,256,2048]{1,2,0:T(8,128)(2,1)}, bf16[8,256,2048]{1,2,0:T(8,128)(2,1)}, u32[]{:S(2)}, u32[]{:S(2)}) collective-permute-start(bf16[8,256,2048]{1,2,0:T(8,128)(2,1)} %fusion.22), channel_id=1, source_target_pairs={{1,0},{2,1},{3,2},{5,4},{6,5},{7,6},{9,8},{10,9},{11,10},{13,12},{... | collective-permute-start | bytes 25165832 | tf_op jit(solution)/shard_map/ppermute | solution.py:12
Sparse Core Ops, SparseCore 0:
  1376.1 167.0 reduce-scatter.1
where the time goes:
time: 1560 us; the launch traced here: 1550 us
  matrix products  476 us (31%)
  local copies, waits for them, and re-layouts  392 us (25%)
  blocking collectives  325 us (21%)
  waiting for transfers between devices  245 us (16%)
  other arithmetic  90.4 us (6%)
    all_to_all x1, blocking collectives, on_device(): lax.all_to_all(volts, 'chan', split_axis=3, concat_axis=0, tiled=True)  325 us
    reduce_scatter x1, waiting for transfers between devices, on_device(): lax.psum_scatter(dedisperse(extended, local_delays, spec_dev, trials, sca...  167 us
    another operation x2, local copies, waits for them, and re-layouts, transform(): shaped = frames_rows.reshape(rows_count, first, second)  104 us
    dot_general x9, matrix products, turn(): jnp.einsum('scb,tc->bst', piece, selector, preferred_element_type=jnp.flo...  82.9 us
    ppermute x2, waiting for transfers between devices, shifted(): return lax.ppermute(array, axis, pairs)  77.6 us
    dot_general x1, matrix products, transform(): section_real = jnp.einsum('rab,ak->rkb', shaped, cos_one, precision=highest)  54.9 us
    add x1, other arithmetic, on_device(): filtered + fir_taps[tap_index][None, None, :] * extended_frames[:, offset...  53 us
    mul x2, local copies, waits for them, and re-layouts, transform(): out_real.reshape(rows_count, nfft // 2) * scale  52.9 us
  transfers between devices with their start and end apart: 3, of which 3 were waited for; matrix products, arithmetic and copies ran while one was open for 0% of the time, Pallas kernels for 0%

commit v1 on v0

--- a/solution.py
+++ b/solution.py
@@ -1,9 +1,20 @@
+import functools
 import math
 
 import jax
 import jax.numpy as jnp
+import numpy as np
 from jax import lax
+from jax.experimental import pallas as pl
+from jax.experimental.pallas import tpu as pltpu
 from jax.sharding import PartitionSpec as P
+
+
+LANES = 128
+GROUP_X = 4
+PAIR = 2
+BF16 = jnp.bfloat16
+F32 = jnp.float32
 
 
 def shifted(array, axis, by):
@@ -74,7 +85,7 @@
     return summed * scale
 
 
-def on_device(samples, fir_taps, beam_y, beam_x, delays):
+def plain_device(samples, fir_taps, beam_y, beam_x, delays):
     dish_dev, total_points = samples.shape
     taps_count, nfft = fir_taps.shape
     spec_dev = total_points // nfft
@@ -126,6 +137,484 @@
     )
 
 
+def real_dft(parts):
+    count = len(parts)
+    if count == 1:
+        return [(parts[0], None)]
+    half = count // 2
+    even = real_dft(parts[0::2])
+    odd = real_dft(parts[1::2])
+    out = [None] * (half + 1)
+    for k in range(half // 2 + 1):
+        even_re, even_im = even[k]
+        odd_re, odd_im = odd[k]
+        if k == 0:
+            out[0] = (even_re + odd_re, None)
+            out[half] = (even_re - odd_re, None)
+        elif 4 * k == count:
+            out[k] = (even_re, -odd_re)
+        else:
+            cos = math.cos(2.0 * math.pi * k / count)
+            sin = math.sin(2.0 * math.pi * k / count)
+            if 8 * k == count:
+                turn_re = (odd_re + odd_im) * cos
+                turn_im = (odd_im - odd_re) * cos
+            else:
+                turn_re = odd_re * cos + odd_im * sin
+                turn_im = odd_im * cos - odd_re * sin
+            out[k] = (even_re + turn_re, even_im + turn_im)
+            out[half - k] = (even_re - turn_re, turn_im - even_im)
+    return out
+
+
+def dft_tables(nfft):
+    radix = nfft // LANES
+    point = np.arange(LANES)[:, None]
+    column = np.arange(LANES)[None, :]
+    scale = 1.0 / math.sqrt(nfft)
+    angle = 2.0 * np.pi * ((point * column) % LANES) / LANES
+    sign = np.where(column < LANES // 2, 1.0, -1.0)
+    cos, sin = np.cos(angle), np.sin(angle)
+    full = np.block([[cos, -sin * sign], [sin, cos * sign]]) * scale
+    low = column < LANES // 2
+    low_angle = 2.0 * np.pi * ((point * radix * column) % nfft) / nfft
+    high_index = radix // 2 + radix * (column - LANES // 2)
+    high_angle = 2.0 * np.pi * ((point * high_index) % nfft) / nfft
+    edge = (
+        np.block(
+            [
+                [np.where(low, np.cos(low_angle), 0.0), np.where(low, -np.sin(low_angle), 0.0)],
+                [np.where(low, 0.0, np.cos(high_angle)), np.where(low, 0.0, -np.sin(high_angle))],
+            ]
+        )
+        * scale
+    )
+    tables = np.stack([edge, full]).astype(np.float32)
+    turn = 2.0 * np.pi * np.arange(radix // 2)[:, None] * np.arange(LANES)[None, :] / nfft
+    twist = np.stack([np.cos(turn), np.sin(turn)]).astype(np.float32)
+    return tables, twist
+
+
+def split(value):
+    high = value.astype(BF16)
+    return high, (value - high.astype(F32)).astype(BF16)
+
+
+def front_kernel(low_spec, taps_count, hist_list, hist_base, peers, pieces, *refs):
+    own = refs[0]
+    hists = refs[1 : 1 + hist_list]
+    taps, twist, mat_high, mat_low, steer = refs[1 + hist_list : 6 + hist_list]
+    outs = refs[6 + hist_list : 6 + hist_list + peers]
+    ships = refs[6 + hist_list + peers : 6 + hist_list + peers + len(pieces)]
+    win, filt, z_high, z_low, volt, sem, ship_sem = refs[6 + hist_list + peers + len(pieces) :]
+    groups, frames, rows, nfft = win.shape
+    slabs = z_high.shape[0]
+    radix = nfft // LANES
+    step = 16
+
+    def fetch(group, index):
+        frame = low_spec - taps_count + 1 + index
+        row_block = pl.ds(group * rows, rows)
+        if frame >= 0:
+            source = own.at[row_block, pl.ds(frame * nfft, nfft)]
+        else:
+            which, place = hist_base[frame]
+            source = hists[which].at[row_block, pl.ds(place * nfft, nfft)]
+        return pltpu.make_async_copy(source, win.at[group, index], sem.at[group, index])
+
+    for group in range(groups):
+        for index in range(frames):
+            fetch(group, index).start()
+
+    def ship(group, which, place):
+        index = pieces[which][0] + place
+        return pltpu.make_async_copy(
+            win.at[group, index],
+            ships[which].at[pl.ds(group * rows, rows), pl.ds(place * nfft, nfft)],
+            ship_sem.at[group, index],
+        )
+
+    every = [(which, place) for which, piece in enumerate(pieces) for place in range(piece[1])]
+
+    def on_group(group, carry):
+        for index in range(frames):
+            fetch(group, index).wait()
+        for which, place in every:
+            ship(group, which, place).start()
+
+        def on_spec(place, carry):
+            def fir(block, carry):
+                block_rows = pl.ds(pl.multiple_of(block * step, step), step)
+                for tile in range(radix):
+                    lanes = slice(tile * LANES, (tile + 1) * LANES)
+                    total = None
+                    for tap in range(taps_count):
+                        piece = win[group, place + taps_count - 1 - tap, block_rows, lanes]
+                        term = piece.astype(F32) * taps[tap : tap + 1, lanes]
+                        total = term if total is None else total + term
+                    filt[block_rows, lanes] = total
+                return carry
+
+            lax.fori_loop(0, rows // step, fir, 0)
+
+            def turn(block, carry):
+                block_rows = pl.ds(pl.multiple_of(block * step, step), step)
+                bins = real_dft(
+                    [filt[block_rows, tile * LANES : (tile + 1) * LANES] for tile in range(radix)]
+                )
+                for slab in range(slabs):
+                    if slab == 0:
+                        z_re, z_im = bins[0][0], bins[radix // 2][0]
+                    else:
+                        x_re, x_im = bins[slab]
+                        cos = twist[0, slab : slab + 1, :]
+                        sin = twist[1, slab : slab + 1, :]
+                        z_re = x_re * cos + x_im * sin
+                        z_im = x_im * cos - x_re * sin
+                    high, low = split(z_re)
+                    z_high[slab, block_rows, 0:LANES] = high
+                    z_low[slab, block_rows, 0:LANES] = low
+                    high, low = split(z_im)
+                    z_high[slab, block_rows, LANES : 2 * LANES] = high
+                    z_low[slab, block_rows, LANES : 2 * LANES] = low
+                return carry
+
+            lax.fori_loop(0, rows // step, turn, 0)
+
+            def product(first, count, which):
+                size = count * rows
+                high = z_high[first : first + count].reshape(size, 2 * LANES)
+                low = z_low[first : first + count].reshape(size, 2 * LANES)
+                value = jnp.dot(high, mat_high[which], preferred_element_type=F32)
+                value += jnp.dot(low, mat_high[which], preferred_element_type=F32)
+                value += jnp.dot(high, mat_low[which], preferred_element_type=F32)
+                volt[first : first + count] = value.astype(BF16).reshape(count, rows, 2 * LANES)
+
+            product(0, 1, 0)
+            batch = 3 if (slabs - 1) % 3 == 0 else 1
+            for first in range(1, slabs, batch):
+                product(first, batch, 1)
+
+            for slab in range(0, slabs, 2):
+                data = jnp.concatenate(
+                    [
+                        jnp.concatenate([volt[at, :, 0:LANES], volt[at, :, LANES:]], axis=0)
+                        for at in (slab, slab + 1)
+                    ],
+                    axis=1,
+                )
+                beams = jnp.dot(steer[...], data, preferred_element_type=F32).astype(BF16)
+                tile_rows = 2 * PAIR * GROUP_X
+                pairs = steer.shape[0] // (peers * tile_rows)
+                beams = beams.reshape(peers, pairs, tile_rows, 2 * LANES)
+                for peer in range(peers):
+                    for pair in range(pairs):
+                        outs[peer][
+                            place, pair, group, :, slab * LANES : (slab + 2) * LANES
+                        ] = beams[peer, pair]
+            return carry
+
+        lax.fori_loop(0, frames - taps_count + 1, on_spec, 0)
+        return carry
+
+    lax.fori_loop(0, groups, on_group, 0)
+    for group in range(groups):
+        for which, place in every:
+            ship(group, which, place).wait()
+
+
+def front(own, hists, hist_base, taps, twist, mat_high, mat_low, steer, low_spec, specs, peers, pairs, pieces):
+    taps_count, nfft = taps.shape
+    dishes = own.shape[0]
+    rows = steer.shape[1] // 2
+    groups = dishes // rows
+    frames = taps_count + specs - 1
+    slabs = nfft // LANES // 2
+    channels = nfft // 2
+    any_space = pl.BlockSpec(memory_space=pl.ANY)
+    vmem = pl.BlockSpec(memory_space=pltpu.VMEM)
+    flops = 2 * specs * dishes * slabs * 3 * (2 * LANES) ** 2 + 2 * specs * groups * slabs * LANES * steer.size
+    return pl.pallas_call(
+        functools.partial(front_kernel, low_spec, taps_count, len(hists), hist_base, peers, pieces),
+        out_shape=[
+            jax.ShapeDtypeStruct((specs, pairs, groups, 2 * PAIR * GROUP_X, channels), BF16)
+            for _ in range(peers)
+        ]
+        + [jax.ShapeDtypeStruct((dishes, count * nfft), BF16) for _, count in pieces],
+        in_specs=[any_space] * (1 + len(hists)) + [vmem] * 5,
+        out_specs=[vmem] * peers + [any_space] * len(pieces),
+        scratch_shapes=[
+            pltpu.VMEM((groups, frames, rows, nfft), BF16),
+            pltpu.VMEM((rows, nfft), F32),
+            pltpu.VMEM((slabs, rows, 2 * LANES), BF16),
+            pltpu.VMEM((slabs, rows, 2 * LANES), BF16),
+            pltpu.VMEM((slabs, rows, 2 * LANES), BF16),
+            pltpu.SemaphoreType.DMA((groups, frames)),
+            pltpu.SemaphoreType.DMA((groups, frames)),
+        ],
+        compiler_params=pltpu.CompilerParams(vmem_limit_bytes=56 * 1024 * 1024),
+        cost_estimate=pl.CostEstimate(
+            flops=flops, bytes_accessed=dishes * nfft * 2 * (frames + specs), transcendentals=0
+        ),
+    )(own, *hists, taps, twist, mat_high, mat_low, steer)
+
+
+def back_kernel(low_spec, specs, span, peers, first, last, *refs):
+    parts = refs[:peers]
+    if last:
+        refs, (early, own) = refs[:-6] + (refs[-1],) + refs[-4:-1], refs[-6:-4]
+    if first:
+        steer, delays, total, p_high, p_low, chosen = refs[peers:]
+        total[...] = jnp.zeros_like(total)
+    else:
+        steer, delays, before, total, p_high, p_low, chosen = refs[peers:]
+        total[...] = before[...]
+    _, pairs, groups, _, channels = parts[0].shape
+    out_rows = steer.shape[0] // 2
+    width = chosen.shape[1]
+    trials = LANES // 2
+    step = 512
+    upper = lax.broadcasted_iota(jnp.int32, (1, LANES), 1) >= trials
+    for place in range(specs):
+        spec = low_spec + place
+        for pair in range(pairs):
+            for start in range(0, channels, step):
+                lanes = slice(start, start + step)
+                data = jnp.concatenate(
+                    [
+                        parts[peer][place, pair, group, :, lanes]
+                        for peer in range(peers)
+                        for group in range(groups)
+                    ],
+                    axis=0,
+                )
+                formed = jnp.dot(steer[...], data, preferred_element_type=F32)
+                power = formed[:out_rows] * formed[:out_rows] + formed[out_rows:] * formed[out_rows:]
+                high, low = split(power)
+                pair_rows = slice(pair * out_rows, (pair + 1) * out_rows)
+                p_high[pair_rows, lanes] = high
+                p_low[pair_rows, lanes] = low
+        odd = spec % 2
+        for tile in range(width // LANES):
+            top = span + odd - 2 * tile
+            wanted = jnp.where(upper, top - 1, top)
+            chosen[:, tile * LANES : (tile + 1) * LANES] = jnp.where(
+                delays[...] == wanted, 1.0, 0.0
+            ).astype(BF16)
+        base = (spec - odd) * trials
+        start = 0
+        while start < width:
+            size = min(2 * LANES, width - start)
+            weights = chosen[:, start : start + size]
+            value = jnp.dot(p_high[...], weights, preferred_element_type=F32)
+            value += jnp.dot(p_low[...], weights, preferred_element_type=F32)
+            total[:, base + start : base + start + size] += value
+            start += size
+    if last:
+        half = total.shape[1] // 2
+        early[...] = total[:, :half]
+        own[...] = total[:, half:]
+
+
+def back(parts, steer, delays, before, low_spec, span, last):
+    peers = len(parts)
+    specs, pairs, _, _, channels = parts[0].shape
+    beams = pairs * steer.shape[0] // 2
+    width = (span + 2) * LANES // 2
+    shape = (beams, 2 * span * LANES // 2)
+    vmem = pl.BlockSpec(memory_space=pltpu.VMEM)
+    first = before is None
+    extra = () if first else (before,)
+    flops = 2 * specs * (pairs * steer.size * channels + 2 * beams * channels * width)
+    return pl.pallas_call(
+        functools.partial(back_kernel, low_spec, specs, span, peers, first, last),
+        out_shape=[jax.ShapeDtypeStruct((beams, shape[1] // 2), F32)] * 2
+        if last
+        else jax.ShapeDtypeStruct(shape, F32),
+        in_specs=[vmem] * (peers + 2 + len(extra)),
+        out_specs=[vmem, vmem] if last else vmem,
+        scratch_shapes=[
+            pltpu.VMEM((beams, channels), BF16),
+            pltpu.VMEM((beams, channels), BF16),
+            pltpu.VMEM((channels, width), BF16),
+        ]
+        + ([pltpu.VMEM(shape, F32)] if last else []),
+        compiler_params=pltpu.CompilerParams(vmem_limit_bytes=48 * 1024 * 1024),
+        cost_estimate=pl.CostEstimate(
+            flops=flops, bytes_accessed=peers * parts[0].size * 2, transcendentals=0
+        ),
+    )(*parts, steer, delays, *extra)
+
+
+def deal_kernel(peers, me, own, came, *refs):
+    outs = refs[:peers]
+    total = refs[peers]
+    beams, width = own.shape
+    side_x = 8 * peers
+    side_p = beams // side_x
+    total[...] = own[...] + came[...]
+    summed = jnp.broadcast_to(jnp.sum(total[...], axis=0, keepdims=True), (8, width))
+    for peer in range(peers):
+        target = lax.rem(me[0] + peer, peers)
+        for at in range(side_p):
+            outs[peer][8 * at : 8 * at + 8, :] = total[
+                pl.ds(pl.multiple_of(at * side_x + target * 8, 8), 8), :
+            ]
+        outs[peer][8 * side_p : 8 * side_p + 8, :] = summed
+
+
+def join_kernel(peers, scale, beams_all, me, *refs):
+    parts = refs[:peers]
+    out = refs[peers]
+    side_p = parts[0].shape[0] // 8 - 1
+    mean = parts[0][8 * side_p : 8 * side_p + 8, :]
+    for peer in range(1, peers):
+        mean = mean + parts[peer][8 * side_p : 8 * side_p + 8, :]
+    mean = mean * (1.0 / beams_all)
+    for peer in range(peers):
+        source = lax.rem(me[0] + peers - peer, peers)
+        for at in range(side_p):
+            value = (parts[peer][8 * at : 8 * at + 8, :] - mean) * scale
+            for row in range(8):
+                out[pl.ds(row * side_p * peers + source * side_p + at, 1), :] = value[row : row + 1, :]
+
+
+def fast_device(samples, fir_taps, beam_y, beam_x, delays):
+    dishes, points = samples.shape
+    taps_count, nfft = fir_taps.shape
+    span = points // nfft
+    side_x, side_y = beam_x.shape[1], beam_y.shape[1]
+    trials, channels = delays.shape
+    peers = lax.axis_size("chan")
+    me = lax.axis_index("chan")
+    side_p = side_y // peers
+    pairs = side_p // PAIR
+    groups = dishes // side_y // GROUP_X
+    radix = nfft // LANES
+
+    chunks = []
+    top, size = span, 1
+    while top > 0:
+        size = 1 if top == 1 else min(size, top - 1)
+        chunks.append((top - size, size))
+        top, size = top - size, 2 * size
+
+    tables, twist = dft_tables(nfft)
+    mat_high = tables.astype(BF16)
+    mat_low = (tables - mat_high.astype(np.float32)).astype(BF16)
+
+    real, imag = beam_y[0], beam_y[1]
+    blocks = jnp.stack([jnp.stack([real, -imag]), jnp.stack([imag, real])])
+    blocks = jnp.concatenate([blocks, blocks], axis=2)
+    blocks = lax.dynamic_slice_in_dim(blocks, me * side_p, side_y, 2)
+    blocks = blocks.transpose(2, 0, 1, 3)[:, :, None, :, None, :]
+    eye = jnp.asarray(np.eye(GROUP_X), BF16)[None, None, :, None, :, None]
+    steer_y = (blocks * eye).reshape(side_y * 2 * GROUP_X, 2 * GROUP_X * side_y)
+
+    count_tm = lax.axis_size("tm")
+    forward = [(i, i + 1) for i in range(count_tm - 1)]
+    bounds = sorted({low - taps_count + 1 for low, _ in chunks[1:]}, reverse=True)
+    bounds = [bound for bound in bounds if bound < 0]
+    bounds = bounds[:2] + bounds[-1:] if len(bounds) > 3 else bounds
+    hists, hist_base, pieces = [], {}, []
+    upper = 0
+    for bound in bounds:
+        for frame in range(bound, upper):
+            hist_base[frame] = (len(pieces), frame - bound)
+        first_low = chunks[0][0] - taps_count + 1
+        pieces.append((span + bound - first_low, upper - bound))
+        upper = bound
+    total = None
+    sent = []
+    for at, (low_spec, specs) in enumerate(chunks):
+        frames = range(low_spec - taps_count + 1, low_spec + specs)
+        used = sorted({hist_base[f][0] for f in frames if f < 0})
+        base = {f: (used.index(hist_base[f][0]), hist_base[f][1]) for f in frames if f < 0}
+        outs = front(
+            samples, [hists[i] for i in used], base, fir_taps, twist, mat_high, mat_low, steer_y,
+            low_spec, specs, peers, pairs, () if at else tuple(pieces),
+        )
+        order = sorted(range(1, peers), key=lambda r: abs(r - peers // 2))
+        got = [outs[0]] + [None] * (peers - 1)
+        for shift in order:
+            got[shift] = lax.ppermute(
+                outs[shift], "chan", [(i, (i + shift) % peers) for i in range(peers)]
+            )
+        sent.append((low_spec, got))
+        if at == 0:
+            for which in range(len(pieces)):
+                hists.append(lax.ppermute(outs[peers + which], "tm", forward))
+    delays, beam_x, sent[-1][1][0] = lax.optimization_barrier((delays, beam_x, sent[-1][1][0]))
+    real, imag = beam_x[0], beam_x[1]
+    blocks = jnp.stack([jnp.stack([real, -imag]), jnp.stack([imag, real])])
+    blocks = blocks.reshape(2, 2, side_x, peers, groups, GROUP_X)[:, :, :, ::-1]
+    blocks = jnp.concatenate([blocks, blocks], axis=3)
+    blocks = lax.dynamic_slice_in_dim(blocks, peers - 1 - me, peers, 3)
+    blocks = blocks.transpose(0, 2, 3, 4, 1, 5)[:, None, :, :, :, None, :, :]
+    eye = jnp.asarray(np.eye(PAIR), BF16)[None, :, None, None, None, :, None, None]
+    steer_x = (blocks * eye).reshape(2 * PAIR * side_x, peers * groups * PAIR * 2 * GROUP_X)
+
+    by_bin = delays.reshape(trials, channels // radix, radix).transpose(2, 1, 0)
+    folded = jnp.concatenate([by_bin[radix // 2 : radix // 2 + 1], by_bin[radix // 2 + 1 :][::-1, ::-1]])
+    ordered = jnp.concatenate([by_bin[: radix // 2], folded], axis=1).reshape(channels, trials)
+    ordered = jnp.concatenate([ordered, ordered], axis=1)
+
+    for low_spec, got in sent:
+        total = back(got, steer_x, ordered, total, low_spec, span, low_spec == 0)
+    early, own = total
+
+    width = span * trials
+    came = lax.ppermute(early, "tm", [(i + 1, i) for i in range(count_tm - 1)])
+    spot = me.reshape(1)
+    smem = pl.BlockSpec(memory_space=pltpu.SMEM)
+    vmem = pl.BlockSpec(memory_space=pltpu.VMEM)
+    rows = 8 * (side_p + 1)
+    dealt = pl.pallas_call(
+        functools.partial(deal_kernel, peers),
+        out_shape=[jax.ShapeDtypeStruct((rows, width), F32) for _ in range(peers)],
+        in_specs=[smem, vmem, vmem],
+        out_specs=[vmem] * peers,
+        scratch_shapes=[pltpu.VMEM(own.shape, F32)],
+        name="deal",
+    )(spot, own, came)
+    joined = [dealt[0]]
+    joined += [None] * (peers - 1)
+    for shift in order:
+        joined[shift] = lax.ppermute(
+            dealt[shift], "chan", [(i, (i + shift) % peers) for i in range(peers)]
+        )
+    series = pl.pallas_call(
+        functools.partial(join_kernel, peers, 1.0 / math.sqrt(channels), side_x * side_y),
+        out_shape=jax.ShapeDtypeStruct((own.shape[0], width), F32),
+        in_specs=[smem] + [vmem] * peers,
+        out_specs=vmem,
+        name="join",
+    )(spot, *joined)
+    return series.reshape(own.shape[0], span, trials)
+
+
+def on_device(samples, fir_taps, beam_y, beam_x, delays):
+    dishes, points = samples.shape
+    taps_count, nfft = fir_taps.shape
+    side_x, side_y = beam_x.shape[1], beam_y.shape[1]
+    trials, channels = delays.shape
+    peers = lax.axis_size("chan")
+    span = points // nfft
+    fits = (
+        dishes % (side_y * GROUP_X) == 0
+        and side_y % (peers * PAIR) == 0
+        and side_x == 8 * peers
+        and 2 * trials == LANES
+        and nfft % (4 * LANES) == 0
+        and channels * 2 == nfft
+        and span % 2 == 0
+        and taps_count - 1 <= span
+    )
+    if fits:
+        return fast_device(samples, fir_taps, beam_y, beam_x, delays)
+    return plain_device(samples, fir_taps, beam_y, beam_x, delays)
+
+
 def solution(mesh):
     return jax.shard_map(
         on_device,

time: 1560 us -> 501 us (0.32)
  matrix products: 476 us -> 0 us
  local copies, waits for them, and re-layouts: 392 us -> 35.5 us
  blocking collectives: 325 us -> 0 us
  starting transfers between devices: 8.82 us -> 146 us
  Pallas kernels: 0 us -> 127 us
  other arithmetic: 90.4 us -> 6.3 us
  waiting for transfers between devices: 245 us -> 181 us
    dot_general x23 -> x0, matrix products: 476 us -> none  [the longest x9 82.9 us: turn(): jnp.einsum('scb,tc->bst', piece, selector, preferred_element_type=jnp.flo...]
    all_to_all x1 -> x0, blocking collectives: 325 us -> none  [on_device(): lax.all_to_all(volts, 'chan', split_axis=3, concat_axis=0, tiled=True)]
    reduce_scatter x1 -> x0, waiting for transfers between devices: 167 us -> none  [on_device(): lax.psum_scatter(dedisperse(extended, local_delays, spec_dev, trials, sca...]
    ppermute x2 -> x39, starting transfers between devices: 8.82 us -> 146 us  [the longest x28 123 us: fast_device(): lax.ppermute(outs[shift], 'chan', [(i, (i + shift) % peers) for i in rang...]
    another operation x3 -> x0, local copies, waits for them, and re-layouts: 129 us -> none  [the longest x2 104 us: transform(): shaped = frames_rows.reshape(rows_count, first, second)]
    pallas_call x0 -> x10, Pallas kernels: none -> 127 us  [the longest x4 95.4 us: front(): pl.pallas_call(functools.partial(front_kernel, low_spec, taps_count, len(...]
    ppermute x2 -> x39, waiting for transfers between devices: 77.6 us -> 181 us  [the longest x1 89.1 us: fast_device(): came = lax.ppermute(early, 'tm', [(i + 1, i) for i in range(count_tm - 1)])]
    mul x4 -> x3, local copies, waits for them, and re-layouts: 105 us -> 3.86 us  [the longest x2 2.84 us: fast_device(): blocks * eye]
  transfers between devices with their start and end apart: 3 -> 39, of which waited for: 3 -> 9; matrix products, arithmetic and copies ran while one was open for 0% -> 4% of each run, Pallas kernels for 0% -> 21%
where the time goes in v1:
time: 501 us; the launch traced here: 497 us
  waiting for transfers between devices  181 us (36%)
  starting transfers between devices  146 us (29%)
  Pallas kernels  127 us (25%)
  local copies, waits for them, and re-layouts  35.5 us (7%)
  other arithmetic  6.3 us (1%)
    ppermute x28, starting transfers between devices, fast_device(): lax.ppermute(outs[shift], 'chan', [(i, (i + shift) % peers) for i in rang...  123 us
    pallas_call x4, Pallas kernels, front(): pl.pallas_call(functools.partial(front_kernel, low_spec, taps_count, len(...  95.4 us
    ppermute x1, waiting for transfers between devices, fast_device(): came = lax.ppermute(early, 'tm', [(i + 1, i) for i in range(count_tm - 1)])  89.1 us
    ppermute x28, waiting for transfers between devices, fast_device(): lax.ppermute(outs[shift], 'chan', [(i, (i + shift) % peers) for i in rang...  87.6 us
    pallas_call x4, Pallas kernels, back(): pl.pallas_call(functools.partial(back_kernel, low_spec, specs, span, peer...  27.5 us
    unnamed x98, local copies, waits for them, and re-layouts  18.4 us
    ppermute x7, starting transfers between devices, fast_device(): lax.ppermute(dealt[shift], 'chan', [(i, (i + shift) % peers) for i in ran...  10.7 us
    ppermute x3, starting transfers between devices, fast_device(): hists.append(lax.ppermute(outs[peers + which], 'tm', forward))  10.2 us
  transfers between devices with their start and end apart: 39, of which 9 were waited for; matrix products, arithmetic and copies ran while one was open for 4% of the time, Pallas kernels for 21%

profile of v1, /device:TPU:0, one launch (start us, length us, event | category | flops | bytes accessed | tf_op | source)
XLA Modules:
  0.0 496.5 jit_solution(12464345678430427448)
XLA Ops:
  0.8 0.9 broadcast_multiply_fusion
  1.8 1.0 mul.41.refs_5_.refs_8_.refs_7_.refs_6_
  2.8 15.2 %shard_map.100 = (bf16[1,2,2,16,2048]{4,3,2,1,0:T(8,128)(2,1)}, bf16[1,2,2,16,2048]{4,3,2,1,0:T(8,128)(2,1)}, bf16[1,2,2,16,2048]{4,3,2,1,0:T(8,128)(2,1)}, bf16...) custom-call(bf16[256,32768]{1,0:T(8,128)(2,1)} %refs_0_.7, ...), custom_call_target="tpu_custom_call" | custom-call | flops 2147483648 | bytes 18874368 | tf_op jit(solution)/shard_map/pallas_call | solution.py:337
  18.0 5.7 %collective-permute-start.1 = (bf16[256,16384]{1,0:T(8,128)(2,1)}, bf16[256,16384]{1,0:T(8,128)(2,1)}, u32[]{:S(2)}, u32[]{:S(2)}) collective-permute-start(bf16[256,16384]{1,0:T(8,128)(2,1)} %get-tuple-element.54), channel_id=1, source_target_pairs={{0,1},{1,2},{2,3},{4,5},{5,6},{6,7},{8,9},{9,10},{10,11},{12,13},{... | collective-permute-start | bytes 25165832 | tf_op jit(solution)/shard_map/ppermute | solution.py:546
  23.8 1.5 collective-permute-start
  25.3 2.9 collective-permute-start.2
  28.2 2.0 collective-permute-start.24
  30.3 1.6 collective-permute-start.25
  31.8 8.8 %collective-permute-done.24.refs_1_ = bf16[1,2,2,16,2048]{4,3,2,1,0:T(8,128)(2,1)S(1)} collective-permute-done((bf16[1,2,2,16,2048]{4,3,2,1,0:T(8,128)(2,1)}, bf16[1,2,2,16,2048]{4,3,2,1,0:T(8,128)(2,1)S(1)}, u32[]{:S(2)}, u32[]{:S(2)}) %collective-permute-start.24) | collective-permute-done | bytes 262176 | tf_op jit(solution)/shard_map/ppermute | solution.py:540
  42.1 1.0 collective-permute-start.27
  43.1 14.8 %collective-permute-done.26.refs_3_ = bf16[1,2,2,16,2048]{4,3,2,1,0:T(8,128)(2,1)S(1)} collective-permute-done((bf16[1,2,2,16,2048]{4,3,2,1,0:T(8,128)(2,1)}, bf16[1,2,2,16,2048]{4,3,2,1,0:T(8,128)(2,1)S(1)}, u32[]{:S(2)}, u32[]{:S(2)}) %collective-permute-start.26) | collective-permute-done | bytes 262176 | tf_op jit(solution)/shard_map/ppermute | solution.py:540
  59.3 9.9 %collective-permute-start.29 = (bf16[1,2,2,16,2048]{4,3,2,1,0:T(8,128)(2,1)}, bf16[1,2,2,16,2048]{4,3,2,1,0:T(8,128)(2,1)S(1)}, u32[]{:S(2)}, u32[]{:S(2)}) collective-permute-start(bf16[1,2,2,16,2048]{4,3,2,1,0:T(8,128)(2,1)} %get-tuple-element.89), channel_id=1, source_target_pairs={{0,24},{4,28},{8,0},{12,4},{16,8},{20,12},{24,16},{28,20},{1,25},{... | collective-permute-start | bytes 786440 | tf_op jit(solution)/shard_map/ppermute | solution.py:540
  69.3 2.2 collective-permute-start.30
  71.4 23.7 %shard_map.103 = (bf16[2,2,2,16,2048]{4,3,2,1,0:T(8,128)(2,1)}, bf16[2,2,2,16,2048]{4,3,2,1,0:T(8,128)(2,1)}, bf16[2,2,2,16,2048]{4,3,2,1,0:T(8,128)(2,1)}, bf16...) custom-call(bf16[256,32768]{1,0:T(8,128)(2,1)} %refs_0_.7, ...), custom_call_target="tpu_custom_call" | custom-call | flops 4294967296 | bytes 23068672 | tf_op jit(solution)/shard_map/pallas_call | solution.py:337
  95.8 2.5 collective-permute-start.17
  100.9 3.6 collective-permute-start.20
  104.5 42.1 %shard_map.102 = (bf16[4,2,2,16,2048]{4,3,2,1,0:T(8,128)(2,1)}, bf16[4,2,2,16,2048]{4,3,2,1,0:T(8,128)(2,1)}, bf16[4,2,2,16,2048]{4,3,2,1,0:T(8,128)(2,1)}, bf16...) custom-call(bf16[256,32768]{1,0:T(8,128)(2,1)} %refs_0_.7, ...), custom_call_target="tpu_custom_call" | custom-call | flops 8589934592 | bytes 31457280 | tf_op jit(solution)/shard_map/pallas_call | solution.py:337
  149.5 4.2 collective-permute-start.21
  154.5 14.4 %shard_map.101 = (bf16[1,2,2,16,2048]{4,3,2,1,0:T(8,128)(2,1)}, bf16[1,2,2,16,2048]{4,3,2,1,0:T(8,128)(2,1)}, bf16[1,2,2,16,2048]{4,3,2,1,0:T(8,128)(2,1)}, bf16...) custom-call(bf16[256,32768]{1,0:T(8,128)(2,1)} %refs_0_.7, ...), custom_call_target="tpu_custom_call" | custom-call | flops 2147483648 | bytes 18874368 | tf_op jit(solution)/shard_map/pallas_call | solution.py:337
  169.1 1.5 collective-permute-start.23
  170.5 10.9 %collective-permute-done.21.refs_5_ = bf16[2,2,2,16,2048]{4,3,2,1,0:T(8,128)(2,1)S(1)} collective-permute-done((bf16[2,2,2,16,2048]{4,3,2,1,0:T(8,128)(2,1)}, bf16[2,2,2,16,2048]{4,3,2,1,0:T(8,128)(2,1)S(1)}, u32[]{:S(2)}, u32[]{:S(2)}) %collective-permute-start.21) | collective-permute-done | bytes 524320 | tf_op jit(solution)/shard_map/ppermute | solution.py:540
  181.4 5.2 %collective-permute-start.4 = (bf16[1,2,2,16,2048]{4,3,2,1,0:T(8,128)(2,1)}, bf16[1,2,2,16,2048]{4,3,2,1,0:T(8,128)(2,1)}, u32[]{:S(2)}, u32[]{:S(2)}) collective-permute-start(bf16[1,2,2,16,2048]{4,3,2,1,0:T(8,128)(2,1)} %get-tuple-element.59), channel_id=1, source_target_pairs={{0,8},{4,12},{8,16},{12,20},{16,24},{20,28},{24,0},{28,4},{1,9},{5... | collective-permute-start | bytes 786440 | tf_op jit(solution)/shard_map/ppermute | solution.py:540
  186.7 2.4 copy.19
  189.0 1.9 slice.32
  190.9 1.9 slice.30
  192.8 1.6 slice.31
  194.4 2.0 rev.7
  196.5 1.3 add_add_fusion
  197.8 1.6 collective-permute-start.12
  199.4 3.7 collective-permute-start.13
  203.1 3.3 collective-permute-start.14
  206.4 1.5 collective-permute-start.16
  208.1 1.3 copy.20
  209.5 1.0 broadcast_multiply_fusion.1
  210.5 1.8 mul.45
  212.3 1.0 copy.24.refs_8_
  213.4 2.0 pad_add_fusion.refs_9_
  215.4 1.2 copy-done.16
  216.6 0.9 copy-done.18
  217.5 0.9 copy-done.20
  218.5 0.9 copy-done.22
  219.4 0.9 copy-done.24
  220.4 0.9 copy-done.26
  221.3 0.9 copy-done.28
  222.3 2.6 shard_map.104.refs_10_
  224.9 0.9 copy-done.31
  226.0 7.7 %shard_map.105.refs_10_ = f32[256,1024]{1,0:T(8,128)S(1)} custom-call(bf16[2,2,2,16,2048]{4,3,2,1,0:T(8,128)(2,1)S(1)} %copy-done.3, bf16[2,2,2,16,2048]{4,3,2,1,0:T(8,128)(2,1)S(1)} %copy-done.5, bf16[2,2,2,16,2048]{4,3,2,1,0:T(8,128)(2,1)S(1)} %copy-done.7, bf16[2,2,2,16,2048]{4,3,2,1,0:T(8,128)(2,1)S(1)} %copy-done.9, ...), custom_call_target="tpu_custom_call" | custom-call | flops 3758096384 | bytes 4194304 | tf_op jit(solution)/shard_map/pallas_call | solution.py:429
  233.7 0.9 copy-done.32
  234.7 53.0 %collective-permute-done.12.refs_3_ = bf16[4,2,2,16,2048]{4,3,2,1,0:T(8,128)(2,1)S(1)} collective-permute-done((bf16[4,2,2,16,2048]{4,3,2,1,0:T(8,128)(2,1)}, bf16[4,2,2,16,2048]{4,3,2,1,0:T(8,128)(2,1)S(1)}, u32[]{:S(2)}, u32[]{:S(2)}) %collective-permute-start.12) | collective-permute-done | bytes 1048608 | tf_op jit(solution)/shard_map/ppermute | solution.py:540
  287.7 44.7 %collective-permute-start.7 = (bf16[1,2,2,16,2048]{4,3,2,1,0:T(8,128)(2,1)S(1)}, bf16[1,2,2,16,2048]{4,3,2,1,0:T(8,128)(2,1)S(1)}, u32[]{:S(2)}, u32[]{:S(2)}) collective-permute-start(bf16[1,2,2,16,2048]{4,3,2,1,0:T(8,128)(2,1)S(1)} %copy-done.46), channel_id=1, source_target_pairs={{0,20},{4,24},{8,28},{12,0},{16,4},{20,8},{24,12},{28,16},{1,21},{... | collective-permute-start | bytes 786440 | tf_op jit(solution)/shard_map/ppermute | solution.py:540
  332.5 32.5 %collective-permute-start.9 = (bf16[1,2,2,16,2048]{4,3,2,1,0:T(8,128)(2,1)S(1)}, bf16[1,2,2,16,2048]{4,3,2,1,0:T(8,128)(2,1)S(1)}, u32[]{:S(2)}, u32[]{:S(2)}) collective-permute-start(bf16[1,2,2,16,2048]{4,3,2,1,0:T(8,128)(2,1)S(1)} %copy-done.44), channel_id=1, source_target_pairs={{0,28},{4,0},{8,4},{12,8},{16,12},{20,16},{24,20},{28,24},{1,29},{... | collective-permute-start | bytes 786440 | tf_op jit(solution)/shard_map/ppermute | solution.py:540
  365.0 13.4 %shard_map.106.refs_10_ = f32[256,1024]{1,0:T(8,128)S(1)} custom-call(bf16[4,2,2,16,2048]{4,3,2,1,0:T(8,128)(2,1)S(1)} %copy-done.30, bf16[4,2,2,16,2048]{4,3,2,1,0:T(8,128)(2,1)S(1)} %collective-permute-done.10.refs_1_, bf16[4,2,2,16,2048]{4,3,2,1,0:T(8,128)(2,1)S(1)} %collective-permute-done.11.refs_2_, ...), custom_call_target="tpu_custom_call" | custom-call | flops 7516192768 | bytes 8388608 | tf_op jit(solution)/shard_map/pallas_call | solution.py:429
  378.5 3.7 shard_map.107
  383.0 1.3 collective-permute-start.31
  384.3 89.1 %collective-permute-done.31.came = f32[256,512]{1,0:T(8,128)S(1)} collective-permute-done((f32[256,512]{1,0:T(8,128)S(1)}, f32[256,512]{1,0:T(8,128)S(1)}, u32[]{:S(2)}, u32[]{:S(2)}) %collective-permute-start.31) | collective-permute-done | bytes 524320 | tf_op jit(solution)/shard_map/ppermute | solution.py:567
  474.3 2.2 deal.1
  476.7 1.9 collective-permute-start.33
  479.6 3.6 collective-permute-start.35
  483.8 2.5 collective-permute-start.37
  486.3 1.2 collective-permute-start.38
  487.8 2.3 collective-permute-done.36.refs_5_
  490.0 1.5 collective-permute-done.38.refs_7_
  492.1 2.4 join.1
  494.5 2.0 copy.25
  (147 shorter events, 15.5 us)
Async XLA Ops:
  18.0 82.9 %collective-permute-start.1 = (bf16[256,16384]{1,0:T(8,128)(2,1)}, bf16[256,16384]{1,0:T(8,128)(2,1)}, u32[]{:S(2)}, u32[]{:S(2)}) collective-permute-start(bf16[256,16384]{1,0:T(8,128)(2,1)} %get-tuple-element.54), channel_id=1, source_target_pairs={{0,1},{1,2},{2,3},{4,5},{5,6},{6,7},{8,9},{9,10},{10,11},{12,13},{... | collective-permute-start | bytes 25165832 | tf_op jit(solution)/shard_map/ppermute | solution.py:546
  23.8 45.5 %collective-permute-start = (bf16[256,8192]{1,0:T(8,128)(2,1)}, bf16[256,8192]{1,0:T(8,128)(2,1)S(1)}, u32[]{:S(2)}, u32[]{:S(2)}) collective-permute-start(bf16[256,8192]{1,0:T(8,128)(2,1)} %get-tuple-element.53), channel_id=1, source_target_pairs={{0,1},{1,2},{2,3},{4,5},{5,6},{6,7},{8,9},{9,10},{10,11},{12,13},{... | collective-permute-start | bytes 12582920 | tf_op jit(solution)/shard_map/ppermute | solution.py:546
  25.3 121.3 %collective-permute-start.2 = (bf16[256,4096]{1,0:T(8,128)(2,1)}, bf16[256,4096]{1,0:T(8,128)(2,1)}, u32[]{:S(2)}, u32[]{:S(2)}) collective-permute-start(bf16[256,4096]{1,0:T(8,128)(2,1)} %get-tuple-element.55), channel_id=1, source_target_pairs={{0,1},{1,2},{2,3},{4,5},{5,6},{6,7},{8,9},{9,10},{10,11},{12,13},{... | collective-permute-start | bytes 6291464 | tf_op jit(solution)/shard_map/ppermute | solution.py:546
  28.2 12.4 %collective-permute-start.24 = (bf16[1,2,2,16,2048]{4,3,2,1,0:T(8,128)(2,1)}, bf16[1,2,2,16,2048]{4,3,2,1,0:T(8,128)(2,1)S(1)}, u32[]{:S(2)}, u32[]{:S(2)}) collective-permute-start(bf16[1,2,2,16,2048]{4,3,2,1,0:T(8,128)(2,1)} %get-tuple-element.84), channel_id=1, source_target_pairs={{0,4},{4,8},{8,12},{12,16},{16,20},{20,24},{24,28},{28,0},{1,5},{5... | collective-permute-start | bytes 786440 | tf_op jit(solution)/shard_map/ppermute | solution.py:540
  30.3 11.1 %collective-permute-start.25 = (bf16[1,2,2,16,2048]{4,3,2,1,0:T(8,128)(2,1)}, bf16[1,2,2,16,2048]{4,3,2,1,0:T(8,128)(2,1)S(1)}, u32[]{:S(2)}, u32[]{:S(2)}) collective-permute-start(bf16[1,2,2,16,2048]{4,3,2,1,0:T(8,128)(2,1)} %get-tuple-element.85), channel_id=1, source_target_pairs={{0,8},{4,12},{8,16},{12,20},{16,24},{20,28},{24,0},{28,4},{1,9},{5... | collective-permute-start | bytes 786440 | tf_op jit(solution)/shard_map/ppermute | solution.py:540
  41.4 16.6 %collective-permute-start.26 = (bf16[1,2,2,16,2048]{4,3,2,1,0:T(8,128)(2,1)}, bf16[1,2,2,16,2048]{4,3,2,1,0:T(8,128)(2,1)S(1)}, u32[]{:S(2)}, u32[]{:S(2)}) collective-permute-start(bf16[1,2,2,16,2048]{4,3,2,1,0:T(8,128)(2,1)} %get-tuple-element.86), channel_id=1, source_target_pairs={{0,12},{4,16},{8,20},{12,24},{16,28},{20,0},{24,4},{28,8},{1,13},{... | collective-permute-start | bytes 786440 | tf_op jit(solution)/shard_map/ppermute | solution.py:540
  42.1 16.6 %collective-permute-start.27 = (bf16[1,2,2,16,2048]{4,3,2,1,0:T(8,128)(2,1)}, bf16[1,2,2,16,2048]{4,3,2,1,0:T(8,128)(2,1)S(1)}, u32[]{:S(2)}, u32[]{:S(2)}) collective-permute-start(bf16[1,2,2,16,2048]{4,3,2,1,0:T(8,128)(2,1)} %get-tuple-element.87), channel_id=1, source_target_pairs={{0,16},{4,20},{8,24},{12,28},{16,0},{20,4},{24,8},{28,12},{1,17},{... | collective-permute-start | bytes 786440 | tf_op jit(solution)/shard_map/ppermute | solution.py:540
  58.6 36.5 %collective-permute-start.28 = (bf16[1,2,2,16,2048]{4,3,2,1,0:T(8,128)(2,1)}, bf16[1,2,2,16,2048]{4,3,2,1,0:T(8,128)(2,1)S(1)}, u32[]{:S(2)}, u32[]{:S(2)}) collective-permute-start(bf16[1,2,2,16,2048]{4,3,2,1,0:T(8,128)(2,1)} %get-tuple-element.88), channel_id=1, source_target_pairs={{0,20},{4,24},{8,28},{12,0},{16,4},{20,8},{24,12},{28,16},{1,21},{... | collective-permute-start | bytes 786440 | tf_op jit(solution)/shard_map/ppermute | solution.py:540
  59.3 39.0 %collective-permute-start.29 = (bf16[1,2,2,16,2048]{4,3,2,1,0:T(8,128)(2,1)}, bf16[1,2,2,16,2048]{4,3,2,1,0:T(8,128)(2,1)S(1)}, u32[]{:S(2)}, u32[]{:S(2)}) collective-permute-start(bf16[1,2,2,16,2048]{4,3,2,1,0:T(8,128)(2,1)} %get-tuple-element.89), channel_id=1, source_target_pairs={{0,24},{4,28},{8,0},{12,4},{16,8},{20,12},{24,16},{28,20},{1,25},{... | collective-permute-start | bytes 786440 | tf_op jit(solution)/shard_map/ppermute | solution.py:540
  69.3 2.2 copy-start.33
  69.3 30.6 %collective-permute-start.30 = (bf16[1,2,2,16,2048]{4,3,2,1,0:T(8,128)(2,1)}, bf16[1,2,2,16,2048]{4,3,2,1,0:T(8,128)(2,1)S(1)}, u32[]{:S(2)}, u32[]{:S(2)}) collective-permute-start(bf16[1,2,2,16,2048]{4,3,2,1,0:T(8,128)(2,1)} %get-tuple-element.90), channel_id=1, source_target_pairs={{0,28},{4,0},{8,4},{12,8},{16,12},{20,16},{24,20},{28,24},{1,29},{... | collective-permute-start | bytes 786440 | tf_op jit(solution)/shard_map/ppermute | solution.py:540
  95.8 51.4 %collective-permute-start.17 = (bf16[2,2,2,16,2048]{4,3,2,1,0:T(8,128)(2,1)}, bf16[2,2,2,16,2048]{4,3,2,1,0:T(8,128)(2,1)S(1)}, u32[]{:S(2)}, u32[]{:S(2)}) collective-permute-start(bf16[2,2,2,16,2048]{4,3,2,1,0:T(8,128)(2,1)} %get-tuple-element.76), channel_id=1, source_target_pairs={{0,4},{4,8},{8,12},{12,16},{16,20},{20,24},{24,28},{28,0},{1,5},{5... | collective-permute-start | bytes 1572872 | tf_op jit(solution)/shard_map/ppermute | solution.py:540
  99.1 49.6 %collective-permute-start.18 = (bf16[2,2,2,16,2048]{4,3,2,1,0:T(8,128)(2,1)}, bf16[2,2,2,16,2048]{4,3,2,1,0:T(8,128)(2,1)S(1)}, u32[]{:S(2)}, u32[]{:S(2)}) collective-permute-start(bf16[2,2,2,16,2048]{4,3,2,1,0:T(8,128)(2,1)} %get-tuple-element.77), channel_id=1, source_target_pairs={{0,8},{4,12},{8,16},{12,20},{16,24},{20,28},{24,0},{28,4},{1,9},{5... | collective-permute-start | bytes 1572872 | tf_op jit(solution)/shard_map/ppermute | solution.py:540
  100.6 53.1 %collective-permute-start.19 = (bf16[2,2,2,16,2048]{4,3,2,1,0:T(8,128)(2,1)}, bf16[2,2,2,16,2048]{4,3,2,1,0:T(8,128)(2,1)S(1)}, u32[]{:S(2)}, u32[]{:S(2)}) collective-permute-start(bf16[2,2,2,16,2048]{4,3,2,1,0:T(8,128)(2,1)} %get-tuple-element.78), channel_id=1, source_target_pairs={{0,12},{4,16},{8,20},{12,24},{16,28},{20,0},{24,4},{28,8},{1,13},{... | collective-permute-start | bytes 1572872 | tf_op jit(solution)/shard_map/ppermute | solution.py:540
  100.9 68.1 %collective-permute-start.20 = (bf16[2,2,2,16,2048]{4,3,2,1,0:T(8,128)(2,1)}, bf16[2,2,2,16,2048]{4,3,2,1,0:T(8,128)(2,1)S(1)}, u32[]{:S(2)}, u32[]{:S(2)}) collective-permute-start(bf16[2,2,2,16,2048]{4,3,2,1,0:T(8,128)(2,1)} %get-tuple-element.79), channel_id=1, source_target_pairs={{0,16},{4,20},{8,24},{12,28},{16,0},{20,4},{24,8},{28,12},{1,17},{... | collective-permute-start | bytes 1572872 | tf_op jit(solution)/shard_map/ppermute | solution.py:540
  146.7 59.7 %collective-permute-start.10 = (bf16[4,2,2,16,2048]{4,3,2,1,0:T(8,128)(2,1)}, bf16[4,2,2,16,2048]{4,3,2,1,0:T(8,128)(2,1)S(1)}, u32[]{:S(2)}, u32[]{:S(2)}) collective-permute-start(bf16[4,2,2,16,2048]{4,3,2,1,0:T(8,128)(2,1)} %get-tuple-element.68), channel_id=1, source_target_pairs={{0,4},{4,8},{8,12},{12,16},{16,20},{20,24},{24,28},{28,0},{1,5},{5... | collective-permute-start | bytes 3145736 | tf_op jit(solution)/shard_map/ppermute | solution.py:540
  148.0 58.4 %collective-permute-start.11 = (bf16[4,2,2,16,2048]{4,3,2,1,0:T(8,128)(2,1)}, bf16[4,2,2,16,2048]{4,3,2,1,0:T(8,128)(2,1)S(1)}, u32[]{:S(2)}, u32[]{:S(2)}) collective-permute-start(bf16[4,2,2,16,2048]{4,3,2,1,0:T(8,128)(2,1)} %get-tuple-element.69), channel_id=1, source_target_pairs={{0,8},{4,12},{8,16},{12,20},{16,24},{20,28},{24,0},{28,4},{1,9},{5... | collective-permute-start | bytes 3145736 | tf_op jit(solution)/shard_map/ppermute | solution.py:540
  149.5 31.9 %collective-permute-start.21 = (bf16[2,2,2,16,2048]{4,3,2,1,0:T(8,128)(2,1)}, bf16[2,2,2,16,2048]{4,3,2,1,0:T(8,128)(2,1)S(1)}, u32[]{:S(2)}, u32[]{:S(2)}) collective-permute-start(bf16[2,2,2,16,2048]{4,3,2,1,0:T(8,128)(2,1)} %get-tuple-element.80), channel_id=1, source_target_pairs={{0,20},{4,24},{8,28},{12,0},{16,4},{20,8},{24,12},{28,16},{1,21},{... | collective-permute-start | bytes 1572872 | tf_op jit(solution)/shard_map/ppermute | solution.py:540
  154.5 26.9 %collective-permute-start.22 = (bf16[2,2,2,16,2048]{4,3,2,1,0:T(8,128)(2,1)}, bf16[2,2,2,16,2048]{4,3,2,1,0:T(8,128)(2,1)}, u32[]{:S(2)}, u32[]{:S(2)}) collective-permute-start(bf16[2,2,2,16,2048]{4,3,2,1,0:T(8,128)(2,1)} %get-tuple-element.81), channel_id=1, source_target_pairs={{0,24},{4,28},{8,0},{12,4},{16,8},{20,12},{24,16},{28,20},{1,25},{... | collective-permute-start | bytes 1572872 | tf_op jit(solution)/shard_map/ppermute | solution.py:540
  154.5 14.4 %copy-start.42 = (bf16[2,64,64]{2,1,0:T(8,128)(2,1)S(1)}, bf16[2,64,64]{2,1,0:T(8,128)(2,1)}, u32[]{:S(2)}) copy-start(bf16[2,64,64]{2,1,0:T(8,128)(2,1)} %param.13) | copy-start | bytes 49156
  169.0 28.8 %copy-start.10 = (bf16[2,2,2,16,2048]{4,3,2,1,0:T(8,128)(2,1)}, bf16[2,2,2,16,2048]{4,3,2,1,0:T(8,128)(2,1)S(1)}, u32[]{:S(2)}) copy-start(bf16[2,2,2,16,2048]{4,3,2,1,0:T(8,128)(2,1)S(1)} %collective-permute-done.20.refs_4_) | copy-start | bytes 1572868
  169.1 28.8 %collective-permute-start.23 = (bf16[2,2,2,16,2048]{4,3,2,1,0:T(8,128)(2,1)}, bf16[2,2,2,16,2048]{4,3,2,1,0:T(8,128)(2,1)}, u32[]{:S(2)}, u32[]{:S(2)}) collective-permute-start(bf16[2,2,2,16,2048]{4,3,2,1,0:T(8,128)(2,1)} %get-tuple-element.82), channel_id=1, source_target_pairs={{0,28},{4,0},{8,4},{12,8},{16,12},{20,16},{24,20},{28,24},{1,29},{... | collective-permute-start | bytes 1572872 | tf_op jit(solution)/shard_map/ppermute | solution.py:540
  181.4 16.4 %copy-start.12 = (bf16[2,2,2,16,2048]{4,3,2,1,0:T(8,128)(2,1)}, bf16[2,2,2,16,2048]{4,3,2,1,0:T(8,128)(2,1)S(1)}, u32[]{:S(2)}) copy-start(bf16[2,2,2,16,2048]{4,3,2,1,0:T(8,128)(2,1)S(1)} %collective-permute-done.21.refs_5_) | copy-start | bytes 1572868
  181.4 18.0 %collective-permute-start.3 = (bf16[1,2,2,16,2048]{4,3,2,1,0:T(8,128)(2,1)}, bf16[1,2,2,16,2048]{4,3,2,1,0:T(8,128)(2,1)}, u32[]{:S(2)}, u32[]{:S(2)}) collective-permute-start(bf16[1,2,2,16,2048]{4,3,2,1,0:T(8,128)(2,1)} %get-tuple-element.58), channel_id=1, source_target_pairs={{0,4},{4,8},{8,12},{12,16},{16,20},{20,24},{24,28},{28,0},{1,5},{5... | collective-permute-start | bytes 786440 | tf_op jit(solution)/shard_map/ppermute | solution.py:540
  181.4 21.7 %collective-permute-start.4 = (bf16[1,2,2,16,2048]{4,3,2,1,0:T(8,128)(2,1)}, bf16[1,2,2,16,2048]{4,3,2,1,0:T(8,128)(2,1)}, u32[]{:S(2)}, u32[]{:S(2)}) collective-permute-start(bf16[1,2,2,16,2048]{4,3,2,1,0:T(8,128)(2,1)} %get-tuple-element.59), channel_id=1, source_target_pairs={{0,8},{4,12},{8,16},{12,20},{16,24},{20,28},{24,0},{28,4},{1,9},{5... | collective-permute-start | bytes 786440 | tf_op jit(solution)/shard_map/ppermute | solution.py:540
  189.0 20.4 %copy-start.43 = (bf16[2,2]{0,1:T(2,128)(2,1)S(1)}, bf16[2,2]{0,1:T(2,128)(2,1)}, u32[]{:S(2)}) copy-start(bf16[2,2]{0,1:T(2,128)(2,1)} %constant.31.clone) | copy-start | bytes 28
  194.4 21.0 %copy-start.14 = (bf16[1,2,2,16,2048]{4,3,2,1,0:T(8,128)(2,1)S(1)}, bf16[1,2,2,16,2048]{4,3,2,1,0:T(8,128)(2,1)}, u32[]{:S(2)}) copy-start(bf16[1,2,2,16,2048]{4,3,2,1,0:T(8,128)(2,1)} %get-tuple-element.83.refs_0_) | copy-start | bytes 786436
  197.8 89.8 %collective-permute-start.12 = (bf16[4,2,2,16,2048]{4,3,2,1,0:T(8,128)(2,1)}, bf16[4,2,2,16,2048]{4,3,2,1,0:T(8,128)(2,1)S(1)}, u32[]{:S(2)}, u32[]{:S(2)}) collective-permute-start(bf16[4,2,2,16,2048]{4,3,2,1,0:T(8,128)(2,1)} %get-tuple-element.70), channel_id=1, source_target_pairs={{0,12},{4,16},{8,20},{12,24},{16,28},{20,0},{24,4},{28,8},{1,13},{... | collective-permute-start | bytes 3145736 | tf_op jit(solution)/shard_map/ppermute | solution.py:540
  199.4 88.2 %collective-permute-start.13 = (bf16[4,2,2,16,2048]{4,3,2,1,0:T(8,128)(2,1)}, bf16[4,2,2,16,2048]{4,3,2,1,0:T(8,128)(2,1)}, u32[]{:S(2)}, u32[]{:S(2)}) collective-permute-start(bf16[4,2,2,16,2048]{4,3,2,1,0:T(8,128)(2,1)} %get-tuple-element.71), channel_id=1, source_target_pairs={{0,16},{4,20},{8,24},{12,28},{16,0},{20,4},{24,8},{28,12},{1,17},{... | collective-permute-start | bytes 3145736 | tf_op jit(solution)/shard_map/ppermute | solution.py:540
  203.1 84.6 %collective-permute-start.14 = (bf16[4,2,2,16,2048]{4,3,2,1,0:T(8,128)(2,1)}, bf16[4,2,2,16,2048]{4,3,2,1,0:T(8,128)(2,1)}, u32[]{:S(2)}, u32[]{:S(2)}) collective-permute-start(bf16[4,2,2,16,2048]{4,3,2,1,0:T(8,128)(2,1)} %get-tuple-element.72), channel_id=1, source_target_pairs={{0,20},{4,24},{8,28},{12,0},{16,4},{20,8},{24,12},{28,16},{1,21},{... | collective-permute-start | bytes 3145736 | tf_op jit(solution)/shard_map/ppermute | solution.py:540
  206.4 126.1 %collective-permute-start.15 = (bf16[4,2,2,16,2048]{4,3,2,1,0:T(8,128)(2,1)}, bf16[4,2,2,16,2048]{4,3,2,1,0:T(8,128)(2,1)}, u32[]{:S(2)}, u32[]{:S(2)}) collective-permute-start(bf16[4,2,2,16,2048]{4,3,2,1,0:T(8,128)(2,1)} %get-tuple-element.73), channel_id=1, source_target_pairs={{0,24},{4,28},{8,0},{12,4},{16,8},{20,12},{24,16},{28,20},{1,25},{... | collective-permute-start | bytes 3145736 | tf_op jit(solution)/shard_map/ppermute | solution.py:540
  206.4 126.1 %collective-permute-start.16 = (bf16[4,2,2,16,2048]{4,3,2,1,0:T(8,128)(2,1)}, bf16[4,2,2,16,2048]{4,3,2,1,0:T(8,128)(2,1)}, u32[]{:S(2)}, u32[]{:S(2)}) collective-permute-start(bf16[4,2,2,16,2048]{4,3,2,1,0:T(8,128)(2,1)} %get-tuple-element.74), channel_id=1, source_target_pairs={{0,28},{4,0},{8,4},{12,8},{16,12},{20,16},{24,20},{28,24},{1,29},{... | collective-permute-start | bytes 3145736 | tf_op jit(solution)/shard_map/ppermute | solution.py:540
  213.3 12.6 %copy-start.3 = (bf16[2,2,2,16,2048]{4,3,2,1,0:T(8,128)(2,1)S(1)}, bf16[2,2,2,16,2048]{4,3,2,1,0:T(8,128)(2,1)}, u32[]{:S(2)}) copy-start(bf16[2,2,2,16,2048]{4,3,2,1,0:T(8,128)(2,1)} %get-tuple-element.75.refs_0_) | copy-start | bytes 1572868
  213.3 12.6 %copy-start.5 = (bf16[2,2,2,16,2048]{4,3,2,1,0:T(8,128)(2,1)S(1)}, bf16[2,2,2,16,2048]{4,3,2,1,0:T(8,128)(2,1)}, u32[]{:S(2)}) copy-start(bf16[2,2,2,16,2048]{4,3,2,1,0:T(8,128)(2,1)} %copy-done.4) | copy-start | bytes 1572868
  213.3 12.6 %copy-start.7 = (bf16[2,2,2,16,2048]{4,3,2,1,0:T(8,128)(2,1)S(1)}, bf16[2,2,2,16,2048]{4,3,2,1,0:T(8,128)(2,1)}, u32[]{:S(2)}) copy-start(bf16[2,2,2,16,2048]{4,3,2,1,0:T(8,128)(2,1)} %copy-done.6) | copy-start | bytes 1572868
  213.3 12.6 %copy-start.9 = (bf16[2,2,2,16,2048]{4,3,2,1,0:T(8,128)(2,1)S(1)}, bf16[2,2,2,16,2048]{4,3,2,1,0:T(8,128)(2,1)}, u32[]{:S(2)}) copy-start(bf16[2,2,2,16,2048]{4,3,2,1,0:T(8,128)(2,1)} %copy-done.8) | copy-start | bytes 1572868
  213.3 12.6 %copy-start.11 = (bf16[2,2,2,16,2048]{4,3,2,1,0:T(8,128)(2,1)S(1)}, bf16[2,2,2,16,2048]{4,3,2,1,0:T(8,128)(2,1)}, u32[]{:S(2)}) copy-start(bf16[2,2,2,16,2048]{4,3,2,1,0:T(8,128)(2,1)} %copy-done.10) | copy-start | bytes 1572868
  213.3 12.6 %copy-start.13 = (bf16[2,2,2,16,2048]{4,3,2,1,0:T(8,128)(2,1)S(1)}, bf16[2,2,2,16,2048]{4,3,2,1,0:T(8,128)(2,1)}, u32[]{:S(2)}) copy-start(bf16[2,2,2,16,2048]{4,3,2,1,0:T(8,128)(2,1)} %copy-done.12) | copy-start | bytes 1572868
  215.4 10.5 %copy-start = (s32[2048,128]{1,0:T(8,128)}, s32[2048,128]{1,0:T(8,128)S(1)}, u32[]{:S(2)}) copy-start(s32[2048,128]{1,0:T(8,128)S(1)} %pad_add_fusion.refs_9_) | copy-start | bytes 3145732
  225.9 61.7 %copy-start.48 = (bf16[1,2,2,16,2048]{4,3,2,1,0:T(8,128)(2,1)S(1)}, bf16[1,2,2,16,2048]{4,3,2,1,0:T(8,128)(2,1)}, u32[]{:S(2)}) copy-start(bf16[1,2,2,16,2048]{4,3,2,1,0:T(8,128)(2,1)} %get-tuple-element.60) | copy-start | bytes 786436
  225.9 61.7 %copy-start.47 = (bf16[1,2,2,16,2048]{4,3,2,1,0:T(8,128)(2,1)S(1)}, bf16[1,2,2,16,2048]{4,3,2,1,0:T(8,128)(2,1)}, u32[]{:S(2)}) copy-start(bf16[1,2,2,16,2048]{4,3,2,1,0:T(8,128)(2,1)} %get-tuple-element.61) | copy-start | bytes 786436
  225.9 61.8 %copy-start.46 = (bf16[1,2,2,16,2048]{4,3,2,1,0:T(8,128)(2,1)S(1)}, bf16[1,2,2,16,2048]{4,3,2,1,0:T(8,128)(2,1)}, u32[]{:S(2)}) copy-start(bf16[1,2,2,16,2048]{4,3,2,1,0:T(8,128)(2,1)} %get-tuple-element.62) | copy-start | bytes 786436
  226.0 106.5 %copy-start.45 = (bf16[1,2,2,16,2048]{4,3,2,1,0:T(8,128)(2,1)S(1)}, bf16[1,2,2,16,2048]{4,3,2,1,0:T(8,128)(2,1)}, u32[]{:S(2)}) copy-start(bf16[1,2,2,16,2048]{4,3,2,1,0:T(8,128)(2,1)} %get-tuple-element.63) | copy-start | bytes 786436
  226.0 106.5 %copy-start.44 = (bf16[1,2,2,16,2048]{4,3,2,1,0:T(8,128)(2,1)S(1)}, bf16[1,2,2,16,2048]{4,3,2,1,0:T(8,128)(2,1)}, u32[]{:S(2)}) copy-start(bf16[1,2,2,16,2048]{4,3,2,1,0:T(8,128)(2,1)} %get-tuple-element.64) | copy-start | bytes 786436
  226.0 139.0 %copy-start.30 = (bf16[4,2,2,16,2048]{4,3,2,1,0:T(8,128)(2,1)S(1)}, bf16[4,2,2,16,2048]{4,3,2,1,0:T(8,128)(2,1)}, u32[]{:S(2)}) copy-start(bf16[4,2,2,16,2048]{4,3,2,1,0:T(8,128)(2,1)} %get-tuple-element.67.refs_0_) | copy-start | bytes 3145732
  287.6 90.8 %collective-permute-start.5 = (bf16[1,2,2,16,2048]{4,3,2,1,0:T(8,128)(2,1)S(1)}, bf16[1,2,2,16,2048]{4,3,2,1,0:T(8,128)(2,1)S(1)}, u32[]{:S(2)}, u32[]{:S(2)}) collective-permute-start(bf16[1,2,2,16,2048]{4,3,2,1,0:T(8,128)(2,1)S(1)} %copy-done.48), channel_id=1, source_target_pairs={{0,12},{4,16},{8,20},{12,24},{16,28},{20,0},{24,4},{28,8},{1,13},{... | collective-permute-start | bytes 786440 | tf_op jit(solution)/shard_map/ppermute | solution.py:540
  287.6 90.8 %collective-permute-start.6 = (bf16[1,2,2,16,2048]{4,3,2,1,0:T(8,128)(2,1)S(1)}, bf16[1,2,2,16,2048]{4,3,2,1,0:T(8,128)(2,1)S(1)}, u32[]{:S(2)}, u32[]{:S(2)}) collective-permute-start(bf16[1,2,2,16,2048]{4,3,2,1,0:T(8,128)(2,1)S(1)} %copy-done.47), channel_id=1, source_target_pairs={{0,16},{4,20},{8,24},{12,28},{16,0},{20,4},{24,8},{28,12},{1,17},{... | collective-permute-start | bytes 786440 | tf_op jit(solution)/shard_map/ppermute | solution.py:540
  287.7 90.7 %collective-permute-start.7 = (bf16[1,2,2,16,2048]{4,3,2,1,0:T(8,128)(2,1)S(1)}, bf16[1,2,2,16,2048]{4,3,2,1,0:T(8,128)(2,1)S(1)}, u32[]{:S(2)}, u32[]{:S(2)}) collective-permute-start(bf16[1,2,2,16,2048]{4,3,2,1,0:T(8,128)(2,1)S(1)} %copy-done.46), channel_id=1, source_target_pairs={{0,20},{4,24},{8,28},{12,0},{16,4},{20,8},{24,12},{28,16},{1,21},{... | collective-permute-start | bytes 786440 | tf_op jit(solution)/shard_map/ppermute | solution.py:540
  332.5 46.0 %collective-permute-start.8 = (bf16[1,2,2,16,2048]{4,3,2,1,0:T(8,128)(2,1)S(1)}, bf16[1,2,2,16,2048]{4,3,2,1,0:T(8,128)(2,1)S(1)}, u32[]{:S(2)}, u32[]{:S(2)}) collective-permute-start(bf16[1,2,2,16,2048]{4,3,2,1,0:T(8,128)(2,1)S(1)} %copy-done.45), channel_id=1, source_target_pairs={{0,24},{4,28},{8,0},{12,4},{16,8},{20,12},{24,16},{28,20},{1,25},{... | collective-permute-start | bytes 786440 | tf_op jit(solution)/shard_map/ppermute | solution.py:540
  332.5 46.0 %collective-permute-start.9 = (bf16[1,2,2,16,2048]{4,3,2,1,0:T(8,128)(2,1)S(1)}, bf16[1,2,2,16,2048]{4,3,2,1,0:T(8,128)(2,1)S(1)}, u32[]{:S(2)}, u32[]{:S(2)}) collective-permute-start(bf16[1,2,2,16,2048]{4,3,2,1,0:T(8,128)(2,1)S(1)} %copy-done.44), channel_id=1, source_target_pairs={{0,28},{4,0},{8,4},{12,8},{16,12},{20,16},{24,20},{28,24},{1,29},{... | collective-permute-start | bytes 786440 | tf_op jit(solution)/shard_map/ppermute | solution.py:540
  365.0 13.5 %copy-start.1 = (s32[2048,128]{1,0:T(8,128)S(1)}, s32[2048,128]{1,0:T(8,128)}, u32[]{:S(2)}) copy-start(s32[2048,128]{1,0:T(8,128)} %copy-done) | copy-start | bytes 3145732
  365.0 13.5 %copy-start.29 = (bf16[1,2,2,16,2048]{4,3,2,1,0:T(8,128)(2,1)S(1)}, bf16[1,2,2,16,2048]{4,3,2,1,0:T(8,128)(2,1)}, u32[]{:S(2)}) copy-start(bf16[1,2,2,16,2048]{4,3,2,1,0:T(8,128)(2,1)} %get-tuple-element.57.refs_0_) | copy-start | bytes 786436
  383.0 90.4 %collective-permute-start.31 = (f32[256,512]{1,0:T(8,128)S(1)}, f32[256,512]{1,0:T(8,128)S(1)}, u32[]{:S(2)}, u32[]{:S(2)}) collective-permute-start(f32[256,512]{1,0:T(8,128)S(1)} %get-tuple-element.92), channel_id=1, source_target_pairs={{1,0},{2,1},{3,2},{5,4},{6,5},{7,6},{9,8},{10,9},{11,10},{13,12},{... | collective-permute-start | bytes 1572872 | tf_op jit(solution)/shard_map/ppermute | solution.py:567
  476.4 7.3 %collective-permute-start.32 = (f32[40,512]{1,0:T(8,128)}, f32[40,512]{1,0:T(8,128)S(1)}, u32[]{:S(2)}, u32[]{:S(2)}) collective-permute-start(f32[40,512]{1,0:T(8,128)} %get-tuple-element.94), channel_id=1, source_target_pairs={{0,4},{4,8},{8,12},{12,16},{16,20},{20,24},{24,28},{28,0},{1,5},{5... | collective-permute-start | bytes 245768 | tf_op jit(solution)/shard_map/ppermute | solution.py:583
  476.7 9.6 %collective-permute-start.33 = (f32[40,512]{1,0:T(8,128)}, f32[40,512]{1,0:T(8,128)S(1)}, u32[]{:S(2)}, u32[]{:S(2)}) collective-permute-start(f32[40,512]{1,0:T(8,128)} %get-tuple-element.95), channel_id=1, source_target_pairs={{0,8},{4,12},{8,16},{12,20},{16,24},{20,28},{24,0},{28,4},{1,9},{5... | collective-permute-start | bytes 245768 | tf_op jit(solution)/shard_map/ppermute | solution.py:583
  478.7 9.1 %collective-permute-start.34 = (f32[40,512]{1,0:T(8,128)}, f32[40,512]{1,0:T(8,128)S(1)}, u32[]{:S(2)}, u32[]{:S(2)}) collective-permute-start(f32[40,512]{1,0:T(8,128)} %get-tuple-element.96), channel_id=1, source_target_pairs={{0,12},{4,16},{8,20},{12,24},{16,28},{20,0},{24,4},{28,8},{1,13},{... | collective-permute-start | bytes 245768 | tf_op jit(solution)/shard_map/ppermute | solution.py:583
  479.6 8.2 %collective-permute-start.35 = (f32[40,512]{1,0:T(8,128)}, f32[40,512]{1,0:T(8,128)S(1)}, u32[]{:S(2)}, u32[]{:S(2)}) collective-permute-start(f32[40,512]{1,0:T(8,128)} %get-tuple-element.97), channel_id=1, source_target_pairs={{0,16},{4,20},{8,24},{12,28},{16,0},{20,4},{24,8},{28,12},{1,17},{... | collective-permute-start | bytes 245768 | tf_op jit(solution)/shard_map/ppermute | solution.py:583
  483.2 6.9 %collective-permute-start.36 = (f32[40,512]{1,0:T(8,128)}, f32[40,512]{1,0:T(8,128)S(1)}, u32[]{:S(2)}, u32[]{:S(2)}) collective-permute-start(f32[40,512]{1,0:T(8,128)} %get-tuple-element.98), channel_id=1, source_target_pairs={{0,20},{4,24},{8,28},{12,0},{16,4},{20,8},{24,12},{28,16},{1,21},{... | collective-permute-start | bytes 245768 | tf_op jit(solution)/shard_map/ppermute | solution.py:583
  483.8 7.7 %copy-start.35 = (f32[40,512]{1,0:T(8,128)}, f32[40,512]{1,0:T(8,128)S(1)}, u32[]{:S(2)}) copy-start(f32[40,512]{1,0:T(8,128)S(1)} %collective-permute-done.32.refs_1_) | copy-start | bytes 245764
  483.8 6.3 %collective-permute-start.37 = (f32[40,512]{1,0:T(8,128)}, f32[40,512]{1,0:T(8,128)S(1)}, u32[]{:S(2)}, u32[]{:S(2)}) collective-permute-start(f32[40,512]{1,0:T(8,128)} %get-tuple-element.99), channel_id=1, source_target_pairs={{0,24},{4,28},{8,0},{12,4},{16,8},{20,12},{24,16},{28,20},{1,25},{... | collective-permute-start | bytes 245768 | tf_op jit(solution)/shard_map/ppermute | solution.py:583
  486.3 5.2 %copy-start.36 = (f32[40,512]{1,0:T(8,128)}, f32[40,512]{1,0:T(8,128)S(1)}, u32[]{:S(2)}) copy-start(f32[40,512]{1,0:T(8,128)S(1)} %collective-permute-done.33.refs_2_) | copy-start | bytes 245764
  486.3 5.2 %collective-permute-start.38 = (f32[40,512]{1,0:T(8,128)}, f32[40,512]{1,0:T(8,128)S(1)}, u32[]{:S(2)}, u32[]{:S(2)}) collective-permute-start(f32[40,512]{1,0:T(8,128)} %get-tuple-element.100), channel_id=1, source_target_pairs={{0,28},{4,0},{8,4},{12,8},{16,12},{20,16},{24,20},{28,24},{1,29},{... | collective-permute-start | bytes 245768 | tf_op jit(solution)/shard_map/ppermute | solution.py:583
  487.7 3.8 copy-start.37
  487.8 3.8 copy-start.38
  (24 other events, 21.4 us)
